TPU v7x, 256 devices: a whole 4x4x8 slice. The times are simulated.
256 devices in a mesh: rep: 2 (over core), shard: 128 (over x, z, y).
Axes of the slice: x: 4, y: 4, z: 8, core: 2. Of those that a mesh axis runs over, the one named last changes fastest.
Arguments:
- grad: bfloat16 [192, 512, 2048], P(None, 'shard'), may hold values from -6 to 6
- momentum: bfloat16 [192, 512, 2048], P(None, 'shard'), may hold values from -6 to 6
- owners: int32 [2, 128, 2], replicated, may hold values from 0 to 192, as said below
Outputs:
- new_momentum: bfloat16 [192, 512, 2048], P(None, 'shard')
- update: bfloat16 [192, 512, 2048], P(None, 'shard')
Inputs may be any that keep to these rules, and one draw needn't show every extreme that they name: `owners`: no matrix index appears twice. In each device's row of 2 slots the entries naming matrices come before the empty ones (value 192). In every draw some device has all 2 slots filled, and some matrices are named by no slot.
All inputs are finite; a program needn't handle non-finite values.
Results may differ from a plain program's by a relative error of at most 0.013.
Values may be sent and summed in bfloat16 or wider, within the bound.
A program may use at most 128 MiB of HBM per device.

v0:
```python
import math
import jax
import jax.numpy as jnp
from jax import lax
from jax.sharding import PartitionSpec as P

R = 512
C = 2048
ITERS = 3
coef_a = 3.4445
coef_b = -4.775
coef_c = 2.0315
mom_decay = 0.95


def newton_schulz(matrix):
    whole = matrix.astype(jnp.float32)
    norm_value = jnp.sqrt(jnp.sum(whole * whole))
    current = (whole / (norm_value + 1e-07)).astype(jnp.bfloat16)
    scaled = None
    for turn_index in range(ITERS):
        gram = lax.dot_general(
            current, current, (((1,), (1,)), ((), ())), preferred_element_type=jnp.float32
        ).astype(jnp.bfloat16)
        square = jnp.dot(gram, gram, preferred_element_type=jnp.float32)
        mixer = (coef_b * gram.astype(jnp.float32) + coef_c * square).astype(jnp.bfloat16)
        result = coef_a * current.astype(jnp.float32) + jnp.dot(
            mixer, current, preferred_element_type=jnp.float32
        )
        if turn_index + 1 < ITERS:
            current = result.astype(jnp.bfloat16)
        else:
            scaled = (0.2 * math.sqrt(max(R, C)) * result).astype(jnp.bfloat16)
    return scaled


def spread_lists(owners, matrix_count, replicas, shard_count):
    devices = replicas * shard_count
    entries = owners.reshape(-1)
    alive = entries < matrix_count
    ordinal = jnp.cumsum(alive.astype(jnp.int32)) - 1
    per_device = (matrix_count + devices - 1) // devices
    target = jnp.where(alive, ordinal, devices * per_device)
    packed = (
        jnp.full((devices * per_device + 1,), matrix_count, jnp.int32)
        .at[target]
        .set(entries)[: devices * per_device]
    )
    return packed.reshape(per_device, shard_count, replicas).transpose(2, 1, 0)


def place_rows(returned, chosen, matrix_count):
    local_rows = returned.shape[1] // chosen.shape[1]
    pieces = returned.reshape(chosen.shape[0] * chosen.shape[1], local_rows, returned.shape[2])
    target = chosen.reshape(-1)
    empty = jnp.zeros((matrix_count, local_rows, returned.shape[2]), jnp.bfloat16)
    return empty.at[target].set(pieces, mode="drop")


def body(grad, momentum, owners):
    fresh = mom_decay * momentum.astype(jnp.float32) + grad.astype(jnp.float32)
    new_momentum = fresh.astype(jnp.bfloat16)
    nesterov = (grad.astype(jnp.float32) + mom_decay * fresh).astype(jnp.bfloat16)
    matrix_count = grad.shape[0]
    local_rows = grad.shape[1]
    width = grad.shape[2]
    replicas = lax.axis_size("rep")
    shard_count = lax.axis_size("shard")
    my_rep = lax.axis_index("rep")
    table = spread_lists(owners, matrix_count, replicas, shard_count)
    slot_count = table.shape[2]
    mine = lax.dynamic_index_in_dim(table, my_rep, 0, keepdims=False)
    chosen = mine.T
    usable = chosen < matrix_count
    taken = jnp.take(nesterov, jnp.minimum(chosen, matrix_count - 1), axis=0)
    outgoing = jnp.where(usable[:, :, None, None], taken, jnp.zeros_like(taken))
    outgoing = outgoing.reshape(slot_count, shard_count * local_rows, width)
    finished = lax.map(
        newton_schulz, lax.all_to_all(outgoing, "shard", split_axis=1, concat_axis=1, tiled=True)
    )
    returned = lax.all_to_all(finished, "shard", split_axis=1, concat_axis=1, tiled=True)
    both = lax.all_gather(returned, "rep", axis=0, tiled=True)
    every_choice = table.transpose(0, 2, 1).reshape(replicas * slot_count, shard_count)
    update = place_rows(both, every_choice, matrix_count)
    return (new_momentum, update)


def solution(mesh):
    placed = (P(None, "shard", None), P(None, "shard", None), P())
    return jax.shard_map(
        body,
        mesh=mesh,
        in_specs=placed,
        out_specs=(P(None, "shard", None), P(None, "shard", None)),
        check_vma=False,
    )
```

profile of v0, /device:TPU:1, one launch (start us, length us, event | category | flops | bytes accessed | tf_op | source)
XLA Modules:
  0.0 297.5 jit_solution(2510085038544679176)
XLA Ops:
  7.2 0.0 all-gather.2.cloned.1.call-start
  7.2 0.7 fusion.27
  7.9 0.8 copy.21
  8.7 0.1 copy.20
  8.9 0.1 reshape.208
  9.0 0.3 reduce-window.9
  9.3 0.1 slice.10
  9.4 0.1 slice_reduce_fusion
  9.5 0.1 add_add_fusion
  9.6 0.2 copy.19
  9.8 0.2 lt.81
  10.0 0.1 reshape.221
  10.1 2.4 scatter_custom_fusion
  12.6 0.1 reshape.206
  12.7 0.2 fusion.18
  12.9 0.2 compare_reduce_fusion
  13.1 7.1 %fusion = (bf16[192,4,2048]{2,1,0:T(4,128)(2,1)S(1)}, bf16[192,4,2048]{2,1,0:T(4,128)(2,1)}) fusion(bf16[192,4,2048]{2,1,0:T(4,128)(2,1)} %param.3, bf16[192,4,2048]{2,1,0:T(4,128)(2,1)} %param.4), kind=kLoop, calls=%fused_computation.5 | loop fusion | flops 12582912 | bytes 12582912 | tf_op jit(solution)/shard_map/convert_element_type | solution.py:63
  20.2 3.5 %gather_fusion = bf16[128,4,2048]{2,1,0:T(4,128)(2,1)} fusion(bf16[192,4,2048]{2,1,0:T(4,128)(2,1)S(1)} %get-tuple-element.15, s32[1024]{0:T(1024)S(1)} %pad_clamp_fusion), kind=kCustom, calls=%fused_computation | custom fusion | bytes 4194816 | tf_op jit(solution)/shard_map/jit(_take)/gather | solution.py:75
  23.7 2.5 gather.7
  26.3 0.1 broadcast_in_dim.51
  26.4 0.1 broadcast_in_dim.52
  26.5 0.1 broadcast_in_dim.54
  26.6 0.1 broadcast_in_dim.55
  26.7 0.3 select_select_fusion
  27.0 5.2 %copy.32 = bf16[1,512,2048]{2,0,1:T(2,128)(2,1)} copy(bf16[1,512,2048]{2,1,0:T(8,128)(2,1)S(1)} %select_select_fusion) | data formatting | bytes 4194304 | tf_op jit(solution)/shard_map/jit(_where)/select_n | solution.py:76
  32.2 0.5 broadcast.218
  32.7 13.1 %reduce.9 = bf16[512,2048]{1,0:T(8,128)(2,1)S(1)} reduce(bf16[512,1,2048]{2,1,0:T(2,128)(2,1)} %bitcast.34, bf16[]{:T(256)} %broadcast.218), dimensions={1}, to_apply=%bitcast.31.reduce_sub_computation | reduce | bytes 4194306
  45.8 2.8 reshape.240
  48.7 65.8 %all_to_all.10 = bf16[128,2,4096]{2,1,0:T(2,128)(2,1)S(1)} all-to-all(bf16[128,2,4096]{2,1,0:T(2,128)(2,1)} %reshape.240), channel_id=1, replica_groups=mesh['rep'=2,'shard'=128] {'shard'}, dimensions={0} | all-to-all | bytes 4194304 | tf_op jit(solution)/shard_map/all_to_all | solution.py:79
  114.4 6.8 %reshape.241 = bf16[512,1,2048]{2,1,0:T(2,128)(2,1)} reshape(bf16[128,2,4096]{2,1,0:T(2,128)(2,1)S(1)} %all_to_all.10) | data formatting | bytes 4194304
  121.2 4.8 %fusion.2 = f32[]{:T(128)} fusion(bf16[1,512,2048]{2,0,1:T(2,128)(2,1)} %bitcast.32), kind=kLoop, calls=%fused_computation.9 | loop fusion | flops 3145727 | bytes 2097156 | tf_op jit(solution)/shard_map/while/body/eval_jaxpr/reduce_sum | solution.py:18
  126.7 3.8 %fusion.5 = bf16[512,2048]{1,0:T(8,128)(2,1)S(1)} fusion(f32[]{:T(128)S(6)} %add.96, bf16[1,512,2048]{2,0,1:T(2,128)(2,1)} %bitcast.33), kind=kLoop, calls=%fused_computation.15 | loop fusion | flops 3145728 | bytes 4194308 | tf_op jit(solution)/shard_map/while/body/eval_jaxpr/convert_element_type | solution.py:19
  130.5 1.3 convolution_convert_fusion.2
  131.8 2.9 add_convert_fusion.1
  134.6 0.0 copy-start.1
  134.7 3.6 %convolution_convert_fusion.1 = bf16[512,512]{1,0:T(8,128)(2,1)S(1)} fusion(bf16[512,2048]{1,0:T(8,128)(2,1)} %add_convert_fusion.1), kind=kOutput, calls=%fused_computation.27 | convolution fusion | flops 1074003968 | bytes 2621440 | tf_op jit(solution)/shard_map/while/body/eval_jaxpr/dot_general | solution.py:22
  138.3 0.0 copy-done.1
  138.3 2.9 add_convert_fusion
  141.2 3.5 %convolution_convert_fusion = bf16[512,512]{1,0:T(8,128)(2,1)S(1)} fusion(bf16[512,2048]{1,0:T(8,128)(2,1)} %add_convert_fusion), kind=kOutput, calls=%fused_computation.26 | convolution fusion | flops 1074003968 | bytes 2621440 | tf_op jit(solution)/shard_map/while/body/eval_jaxpr/dot_general | solution.py:22
  144.7 3.8 %fusion.4 = bf16[1,512,2048]{2,1,0:T(8,128)(2,1)S(1)} fusion(bf16[512,2048]{1,0:T(8,128)(2,1)} %add_convert_fusion, bf16[512,512]{1,0:T(8,128)(2,1)S(1)} %convolution_convert_fusion), kind=kOutput, calls=%fused_computation.14 | convolution fusion | flops 1348730880 | bytes 4718592 | tf_op jit(solution)/shard_map/while/body/eval_jaxpr/dot_general | solution.py:27
  148.5 5.4 %copy.31 = bf16[1,512,2048]{2,0,1:T(2,128)(2,1)} copy(bf16[1,512,2048]{2,1,0:T(8,128)(2,1)S(1)} %fusion.4) | data formatting | bytes 4194304 | tf_op jit(solution)/shard_map/while/body/jit(dynamic_update_index_in_dim)/broadcast_in_dim | solution.py:78
  153.9 13.1 %reduce.10 = bf16[512,2048]{1,0:T(8,128)(2,1)S(1)} reduce(bf16[512,1,2048]{2,1,0:T(2,128)(2,1)} %bitcast.35, bf16[]{:T(256)} %broadcast.218), dimensions={1}, to_apply=%bitcast.30.reduce_sub_computation | reduce | bytes 4194306
  167.0 2.8 reshape.242
  169.9 58.7 %all_to_all.11 = bf16[128,2,4096]{2,1,0:T(2,128)(2,1)S(1)} all-to-all(bf16[128,2,4096]{2,1,0:T(2,128)(2,1)} %reshape.242), channel_id=1, replica_groups=mesh['rep'=2,'shard'=128] {'shard'}, dimensions={0} | all-to-all | bytes 4194304 | tf_op jit(solution)/shard_map/all_to_all | solution.py:81
  228.6 6.8 %reshape.243 = bf16[512,1,2048]{2,1,0:T(2,128)(2,1)} reshape(bf16[128,2,4096]{2,1,0:T(2,128)(2,1)S(1)} %all_to_all.11) | data formatting | bytes 4194304
  235.3 4.8 %copy.26 = bf16[1,512,2048]{2,1,0:T(8,128)(2,1)} copy(bf16[1,512,2048]{2,0,1:T(2,128)(2,1)} %bitcast.36) | data formatting | bytes 4194304 | tf_op jit(solution)/shard_map/all_to_all | solution.py:81
  240.1 0.0 all-gather.2.cloned.1.call-update
  240.1 0.1 copy.22
  240.2 17.8 %all-gather.2.cloned.1.call-done = bf16[2,512,2048]{2,1,0:T(8,128)(2,1)} async-done(((bf16[1,512,2048]{2,1,0:T(8,128)(2,1)}), bf16[2,512,2048]{2,1,0:T(8,128)(2,1)}) %all-gather.2.cloned.1.call-update) | async-done | bytes 4194320 | tf_op jit(solution)/shard_map/all_gather | solution.py:82
  258.0 7.2 %reshape.229 = bf16[256,4,2048]{2,1,0:T(4,128)(2,1)} reshape(bf16[2,512,2048]{2,1,0:T(8,128)(2,1)} %all-gather.2.cloned.1.call-done) | data formatting | bytes 8388608 | tf_op jit(solution)/shard_map/reshape | solution.py:54
  265.2 1.6 broadcast_in_dim.48
  266.8 22.2 %scatter_fusion = bf16[192,4,2048]{2,1,0:T(4,128)(2,1)S(1)} fusion(bf16[192,4,2048]{2,1,0:T(4,128)(2,1)S(1)} %broadcast_in_dim.48, s32[256]{0:T(256)S(1)} %bitcast.39, bf16[256,4,2048]{2,1,0:T(4,128)(2,1)} %reshape.229), kind=kCustom, calls=%fused_computation.2 | custom fusion | bytes 12583936 | tf_op jit(solution)/shard_map/scatter | solution.py:57
  289.0 0.0 copy-start
  289.0 1.7 copy-done
  (5 shorter events, 0.1 us)
Async XLA Ops:
  7.2 250.8 %all-gather.2.cloned.1.call-start = ((), (), s32[]{:S(2)}) async-start(), calls=%async_computation.2 | async-start | bytes 6291456 | tf_op jit(solution)/shard_map/all_gather | solution.py:82
  134.6 3.7 %copy-start.1 = (bf16[512,2048]{1,0:T(8,128)(2,1)S(1)}, bf16[512,2048]{1,0:T(8,128)(2,1)}, u32[]{:S(2)}) copy-start(bf16[512,2048]{1,0:T(8,128)(2,1)} %add_convert_fusion.1) | copy-start | bytes 6291460
  289.0 1.7 copy-start
Sparse Core Ops, SparseCore 0:
  240.3 17.6 all-gather.1
where the time goes:
time: 299 us; the launch traced here: 298 us
  blocking collectives  124 us (41%)
  local copies, waits for them, and re-layouts  78.6 us (26%)
  other arithmetic  43.7 us (15%)
  matrix products  18 us (6%)
  waiting for transfers between devices  17.8 us (6%)
  between operations  14.9 us (5%)
    all_to_all x1, blocking collectives, body(): lax.all_to_all(outgoing, 'shard', split_axis=1, concat_axis=1, tiled=True)  65.8 us
    all_to_all x1, blocking collectives, body(): lax.all_to_all(finished, 'shard', split_axis=1, concat_axis=1, tiled=True)  58.7 us
    unnamed x2, other arithmetic  26.2 us
    scatter x1, local copies, waits for them, and re-layouts, place_rows(): return empty.at[target].set(pieces, mode='drop')  22.2 us
    unnamed x10, local copies, waits for them, and re-layouts  22.2 us
    all_gather x1, waiting for transfers between devices, body(): both = lax.all_gather(returned, 'rep', axis=0, tiled=True)  17.8 us
    dot_general x3, matrix products, newton_schulz(): jnp.dot(mixer, current, preferred_element_type=jnp.float32)  9.57 us
    dot_general x3, matrix products, newton_schulz(): lax.dot_general(current, current, (((1,), (1,)), ((), ())), preferred_ele...  8.43 us
  transfers between devices with their start and end apart: 1, of which 1 were waited for; matrix products, arithmetic and copies ran while one was open for 0% of the time, Pallas kernels for 0%

commit v1 on v0

--- a/solution.py
+++ b/solution.py
@@ -79,7 +79,8 @@
         newton_schulz, lax.all_to_all(outgoing, "shard", split_axis=1, concat_axis=1, tiled=True)
     )
     returned = lax.all_to_all(finished, "shard", split_axis=1, concat_axis=1, tiled=True)
-    both = lax.all_gather(returned, "rep", axis=0, tiled=True)
+    sent = jnp.stack([returned] * lax.axis_size("rep"))
+    both = jnp.concatenate(lax.all_to_all(sent, "rep", 0, 0), axis=0)
     every_choice = table.transpose(0, 2, 1).reshape(replicas * slot_count, shard_count)
     update = place_rows(both, every_choice, matrix_count)
     return (new_momentum, update)

time: 299 us -> 279 us (0.933)
  blocking collectives: 124 us -> 77.7 us
  waiting for transfers between devices: 17.8 us -> 49 us
  between operations: 14.9 us -> 1.54 us
  starting transfers between devices: 0.04 us -> 9.61 us
    all_to_all x0 -> x1, waiting for transfers between devices: none -> 49 us  [body(): lax.all_to_all(finished, 'shard', split_axis=1, concat_axis=1, tiled=True)]
    all_to_all x1, blocking collectives: 58.7 us -> 11.9 us  [body(): both = jnp.concatenate(lax.all_to_all(sent, 'rep', 0, 0), axis=0)]
    all_gather x1 -> x0, waiting for transfers between devices: 17.8 us -> none  [body(): both = lax.all_gather(returned, 'rep', axis=0, tiled=True)]
    all_to_all x0 -> x1, starting transfers between devices: none -> 9.61 us  [body(): lax.all_to_all(finished, 'shard', split_axis=1, concat_axis=1, tiled=True)]
    another operation x1 -> x2, local copies, waits for them, and re-layouts: 0.12 us -> 7.31 us  [the longest x1 7.19 us: place_rows(): returned.reshape(chosen.shape[0] * chosen.shape[1], local_rows, returned....]
    reshape x1 -> x0, local copies, waits for them, and re-layouts: 7.19 us -> none  [place_rows(): returned.reshape(chosen.shape[0] * chosen.shape[1], local_rows, returned....]
    all_to_all x1 -> x0, local copies, waits for them, and re-layouts: 4.78 us -> none  [body(): lax.all_to_all(finished, 'shard', split_axis=1, concat_axis=1, tiled=True)]
    unnamed x10 -> x11, local copies, waits for them, and re-layouts: 22.2 us -> 25.6 us
where the time goes in v1:
time: 279 us; the launch traced here: 277 us
  blocking collectives  77.7 us (28%)
  local copies, waits for them, and re-layouts  77.2 us (28%)
  waiting for transfers between devices  49 us (18%)
  other arithmetic  44.1 us (16%)
  matrix products  18 us (6%)
  starting transfers between devices  9.61 us (3%)
    all_to_all x1, blocking collectives, body(): lax.all_to_all(outgoing, 'shard', split_axis=1, concat_axis=1, tiled=True)  65.8 us
    all_to_all x1, waiting for transfers between devices, body(): lax.all_to_all(finished, 'shard', split_axis=1, concat_axis=1, tiled=True)  49 us
    unnamed x2, other arithmetic  26.2 us
    unnamed x11, local copies, waits for them, and re-layouts  25.6 us
    scatter x1, local copies, waits for them, and re-layouts, place_rows(): return empty.at[target].set(pieces, mode='drop')  22.2 us
    all_to_all x1, blocking collectives, body(): both = jnp.concatenate(lax.all_to_all(sent, 'rep', 0, 0), axis=0)  11.9 us
    all_to_all x1, starting transfers between devices, body(): lax.all_to_all(finished, 'shard', split_axis=1, concat_axis=1, tiled=True)  9.61 us
    dot_general x3, matrix products, newton_schulz(): jnp.dot(mixer, current, preferred_element_type=jnp.float32)  9.56 us
  transfers between devices with their start and end apart: 1, of which 1 were waited for; matrix products, arithmetic and copies ran while one was open for 0% of the time, Pallas kernels for 0%

profile of v1, /device:TPU:1, one launch (start us, length us, event | category | flops | bytes accessed | tf_op | source)
XLA Modules:
  0.0 277.2 jit_solution(11509632346757871590)
XLA Ops:
  0.6 0.7 fusion.27
  1.3 0.8 copy.20
  2.1 0.1 copy.19
  2.3 0.1 reshape.204
  2.4 0.3 reduce-window.9
  2.7 0.1 slice.10
  2.8 0.1 slice_reduce_fusion
  3.0 0.1 add_add_fusion
  3.0 0.2 copy.18
  3.2 0.2 lt.81
  3.4 0.1 reshape.217
  3.5 2.4 scatter_custom_fusion
  6.0 0.1 reshape.203
  6.1 0.2 fusion.18
  6.3 0.2 compare_reduce_fusion
  6.5 7.1 %fusion = (bf16[192,4,2048]{2,1,0:T(4,128)(2,1)S(1)}, bf16[192,4,2048]{2,1,0:T(4,128)(2,1)}) fusion(bf16[192,4,2048]{2,1,0:T(4,128)(2,1)} %param.3, bf16[192,4,2048]{2,1,0:T(4,128)(2,1)} %param.4), kind=kLoop, calls=%fused_computation.5 | loop fusion | flops 12582912 | bytes 12582912 | tf_op jit(solution)/shard_map/convert_element_type | solution.py:63
  13.6 3.5 %gather_fusion = bf16[128,4,2048]{2,1,0:T(4,128)(2,1)} fusion(bf16[192,4,2048]{2,1,0:T(4,128)(2,1)S(1)} %get-tuple-element.15, s32[1024]{0:T(1024)S(1)} %pad_clamp_fusion), kind=kCustom, calls=%fused_computation | custom fusion | bytes 4194816 | tf_op jit(solution)/shard_map/jit(_take)/gather | solution.py:75
  17.2 2.5 gather.7
  19.7 0.1 broadcast_in_dim.51
  19.8 0.1 broadcast_in_dim.52
  19.9 0.1 broadcast_in_dim.54
  20.0 0.1 broadcast_in_dim.55
  20.1 0.3 select_select_fusion
  20.5 5.2 %copy.33 = bf16[1,512,2048]{2,0,1:T(2,128)(2,1)} copy(bf16[1,512,2048]{2,1,0:T(8,128)(2,1)S(1)} %select_select_fusion) | data formatting | bytes 4194304 | tf_op jit(solution)/shard_map/jit(_where)/select_n | solution.py:76
  25.6 0.5 broadcast.218
  26.1 13.1 %reduce.9 = bf16[512,2048]{1,0:T(8,128)(2,1)S(1)} reduce(bf16[512,1,2048]{2,1,0:T(2,128)(2,1)} %bitcast.39, bf16[]{:T(256)} %broadcast.218), dimensions={1}, to_apply=%bitcast.36.reduce_sub_computation | reduce | bytes 4194306
  39.3 2.8 %reshape.236 = bf16[128,2,4096]{2,1,0:T(2,128)(2,1)} reshape(bf16[512,2048]{1,0:T(8,128)(2,1)S(1)} %reduce.9) | data formatting | bytes 4194304
  42.1 65.8 %all_to_all.15 = bf16[128,2,4096]{2,1,0:T(2,128)(2,1)S(1)} all-to-all(bf16[128,2,4096]{2,1,0:T(2,128)(2,1)} %reshape.236), channel_id=1, replica_groups=mesh['rep'=2,'shard'=128] {'shard'}, dimensions={0} | all-to-all | bytes 4194304 | tf_op jit(solution)/shard_map/all_to_all | solution.py:79
  107.9 6.8 %reshape.237 = bf16[512,1,2048]{2,1,0:T(2,128)(2,1)} reshape(bf16[128,2,4096]{2,1,0:T(2,128)(2,1)S(1)} %all_to_all.15) | data formatting | bytes 4194304
  114.6 4.8 %fusion.2 = f32[]{:T(128)} fusion(bf16[1,512,2048]{2,0,1:T(2,128)(2,1)} %bitcast.37), kind=kLoop, calls=%fused_computation.9 | loop fusion | flops 3145727 | bytes 2097156 | tf_op jit(solution)/shard_map/while/body/eval_jaxpr/reduce_sum | solution.py:18
  120.1 3.8 %fusion.5 = bf16[512,2048]{1,0:T(8,128)(2,1)S(1)} fusion(f32[]{:T(128)S(6)} %add.96, bf16[1,512,2048]{2,0,1:T(2,128)(2,1)} %bitcast.38), kind=kLoop, calls=%fused_computation.16 | loop fusion | flops 3145728 | bytes 4194308 | tf_op jit(solution)/shard_map/while/body/eval_jaxpr/convert_element_type | solution.py:19
  123.9 1.3 convolution_convert_fusion.2
  125.2 2.9 %add_convert_fusion.1 = bf16[512,2048]{1,0:T(8,128)(2,1)} fusion(bf16[512,2048]{1,0:T(8,128)(2,1)S(1)} %fusion.5, bf16[512,512]{1,0:T(8,128)(2,1)S(1)} %convolution_convert_fusion.2), kind=kOutput, calls=%fused_computation.14 | convolution fusion | flops 1347682304 | bytes 4718592 | tf_op jit(solution)/shard_map/while/body/eval_jaxpr/dot_general | solution.py:27
  128.1 0.0 copy-start.1
  128.1 3.6 %convolution_convert_fusion.1 = bf16[512,512]{1,0:T(8,128)(2,1)S(1)} fusion(bf16[512,2048]{1,0:T(8,128)(2,1)} %add_convert_fusion.1), kind=kOutput, calls=%fused_computation.29 | convolution fusion | flops 1074003968 | bytes 2621440 | tf_op jit(solution)/shard_map/while/body/eval_jaxpr/dot_general | solution.py:22
  131.7 0.0 copy-done.1
  131.7 2.9 %add_convert_fusion = bf16[512,2048]{1,0:T(8,128)(2,1)} fusion(bf16[512,2048]{1,0:T(8,128)(2,1)S(1)} %copy-done.1, bf16[512,512]{1,0:T(8,128)(2,1)S(1)} %convolution_convert_fusion.1), kind=kOutput, calls=%fused_computation.13 | convolution fusion | flops 1347682304 | bytes 4718592 | tf_op jit(solution)/shard_map/while/body/eval_jaxpr/dot_general | solution.py:27
  134.6 3.5 %convolution_convert_fusion = bf16[512,512]{1,0:T(8,128)(2,1)S(1)} fusion(bf16[512,2048]{1,0:T(8,128)(2,1)} %add_convert_fusion), kind=kOutput, calls=%fused_computation.28 | convolution fusion | flops 1074003968 | bytes 2621440 | tf_op jit(solution)/shard_map/while/body/eval_jaxpr/dot_general | solution.py:22
  138.1 3.8 %fusion.4 = bf16[1,512,2048]{2,1,0:T(8,128)(2,1)S(1)} fusion(bf16[512,2048]{1,0:T(8,128)(2,1)} %add_convert_fusion, bf16[512,512]{1,0:T(8,128)(2,1)S(1)} %convolution_convert_fusion), kind=kOutput, calls=%fused_computation.15 | convolution fusion | flops 1348730880 | bytes 4718592 | tf_op jit(solution)/shard_map/while/body/eval_jaxpr/dot_general | solution.py:27
  141.9 5.4 %copy.32 = bf16[1,512,2048]{2,0,1:T(2,128)(2,1)} copy(bf16[1,512,2048]{2,1,0:T(8,128)(2,1)S(1)} %fusion.4) | data formatting | bytes 4194304 | tf_op jit(solution)/shard_map/while/body/jit(dynamic_update_index_in_dim)/broadcast_in_dim | solution.py:78
  147.3 13.1 %reduce.10 = bf16[512,2048]{1,0:T(8,128)(2,1)S(1)} reduce(bf16[512,1,2048]{2,1,0:T(2,128)(2,1)} %bitcast.40, bf16[]{:T(256)} %broadcast.218), dimensions={1}, to_apply=%bitcast.35.reduce_sub_computation | reduce | bytes 4194306
  160.4 2.8 %reshape.238 = bf16[128,2,4096]{2,1,0:T(2,128)(2,1)} reshape(bf16[512,2048]{1,0:T(8,128)(2,1)S(1)} %reduce.10) | data formatting | bytes 4194304
  163.3 9.6 %all-to-all-start.1 = ((bf16[128,2,4096]{2,1,0:T(2,128)(2,1)}), bf16[128,2,4096]{2,1,0:T(2,128)(2,1)S(1)}, u32[]{:S(2)}, u32[]{:S(2)}) async-start(bf16[128,2,4096]{2,1,0:T(2,128)(2,1)} %reshape.238), calls=%async_computation.1 | async-start | bytes 4194304 | tf_op jit(solution)/shard_map/all_to_all | solution.py:81
  172.9 0.1 copy.21
  172.9 49.0 %all-to-all-done.1 = bf16[128,2,4096]{2,1,0:T(2,128)(2,1)S(1)} async-done(((bf16[128,2,4096]{2,1,0:T(2,128)(2,1)}), bf16[128,2,4096]{2,1,0:T(2,128)(2,1)S(1)}, u32[]{:S(2)}, u32[]{:S(2)}) %all-to-all-start.1) | async-done | bytes 2097184 | tf_op jit(solution)/shard_map/all_to_all | solution.py:81
  222.0 6.8 %reshape.239 = bf16[512,1,2048]{2,1,0:T(2,128)(2,1)} reshape(bf16[128,2,4096]{2,1,0:T(2,128)(2,1)S(1)} %all-to-all-done.1) | data formatting | bytes 4194304
  228.8 3.5 %copy.31 = bf16[1,512,2048]{2,1,0:T(8,128)(2,1)S(1)} copy(bf16[1,512,2048]{2,0,1:T(2,128)(2,1)} %bitcast.41) | data formatting | bytes 4194304
  232.2 0.4 pad_maximum_fusion
  232.6 11.9 %all_to_all.16 = bf16[2,1,512,2048]{3,2,1,0:T(8,128)(2,1)} all-to-all(bf16[2,1,512,2048]{3,2,1,0:T(8,128)(2,1)S(1)} %pad_maximum_fusion), channel_id=1, replica_groups=mesh['rep'=2,'shard'=128] {'rep'}, dimensions={0} | all-to-all | bytes 8388608 | tf_op jit(solution)/shard_map/all_to_all | solution.py:83
  244.5 7.2 %reshape.225 = bf16[256,4,2048]{2,1,0:T(4,128)(2,1)} reshape(bf16[2,1,512,2048]{3,2,1,0:T(8,128)(2,1)} %all_to_all.16) | data formatting | bytes 8388608 | tf_op jit(solution)/shard_map/reshape;reshape | solution.py:54
  251.7 1.6 broadcast_in_dim.48
  253.3 22.2 %scatter_fusion = bf16[192,4,2048]{2,1,0:T(4,128)(2,1)S(1)} fusion(bf16[192,4,2048]{2,1,0:T(4,128)(2,1)S(1)} %broadcast_in_dim.48, s32[256]{0:T(256)S(1)} %bitcast.45, bf16[256,4,2048]{2,1,0:T(4,128)(2,1)} %reshape.225), kind=kCustom, calls=%fused_computation.2 | custom fusion | bytes 12583936 | tf_op jit(solution)/shard_map/scatter | solution.py:57
  275.6 0.0 copy-start
  275.6 1.7 copy-done
  (5 shorter events, 0.1 us)
Async XLA Ops:
  128.1 3.7 %copy-start.1 = (bf16[512,2048]{1,0:T(8,128)(2,1)S(1)}, bf16[512,2048]{1,0:T(8,128)(2,1)}, u32[]{:S(2)}) copy-start(bf16[512,2048]{1,0:T(8,128)(2,1)} %add_convert_fusion.1) | copy-start | bytes 6291460
  163.3 58.7 %all-to-all-start.1 = ((bf16[128,2,4096]{2,1,0:T(2,128)(2,1)}), bf16[128,2,4096]{2,1,0:T(2,128)(2,1)S(1)}, u32[]{:S(2)}, u32[]{:S(2)}) async-start(bf16[128,2,4096]{2,1,0:T(2,128)(2,1)} %reshape.238), calls=%async_computation.1 | async-start | bytes 4194304 | tf_op jit(solution)/shard_map/all_to_all | solution.py:81
  275.6 1.7 copy-start
